TPU v7x, 32 devices: a whole 2x2x4 slice. The times are simulated.
32 devices in a mesh: section: 2 (over y), dp: 4 (over x, core), mp: 4 (over z).
Axes of the slice: x: 2, y: 2, z: 4, core: 2. Of those that a mesh axis runs over, the one named last changes fastest.
Arguments:
- activations: bfloat16 [2, 256, 4096], P(None, 'dp'), may hold values from -6 to 6
- cotangent: bfloat16 [2, 256, 4096], P(None, 'dp'), may hold values from -6 to 6
- norm_gain: float32 [2, 4096], P('section'), may hold values from 0.1 to 1.9
- w_up: bfloat16 [2, 4096, 8192], P('section', 'dp', 'mp'), may hold values from -0.09375 to 0.09375
- w_down: bfloat16 [2, 4096, 8192], P('section', 'dp', 'mp'), may hold values from -0.0625 to 0.0625
- gram_left: float32 [2, 128, 512, 512], P('section', ('dp', 'mp')), as said below
- gram_right: float32 [2, 128, 512, 512], P('section', ('dp', 'mp')), as said below
- root_left: bfloat16 [2, 128, 512, 512], P('section', ('dp', 'mp'))
- root_right: bfloat16 [2, 128, 512, 512], P('section', ('dp', 'mp'))
- owner_slot: int32 [2, 16, 8], replicated, may hold values from 0 to 127, as said below
- eighth: int32 [2, 16, 8], replicated, may hold values from 0 to 7, as said below
- refresh_phase: int32 [1], replicated, may hold values from 0 to 999999
Outputs:
- new_gram_left: float32 [2, 128, 512, 512], P('section', ('dp', 'mp'))
- new_gram_right: float32 [2, 128, 512, 512], P('section', ('dp', 'mp'))
- new_root_left: bfloat16 [2, 128, 512, 512], P('section', ('dp', 'mp'))
- new_root_right: bfloat16 [2, 128, 512, 512], P('section', ('dp', 'mp'))
- update_blocks: bfloat16 [2, 128, 512, 512], P('section', ('dp', 'mp'))
Inputs may be any that keep to these rules, and one draw needn't show every extreme that they name: `owner_slot`: for each section, a permutation of the 128 slots; the block of flat index f = i * 8 + j goes to a slot t with (t // 8) % (4) == f // 32. `eighth`: in each section and each run of 32 consecutive flat block indices, every value is taken by exactly 4 blocks. `gram_left`: symmetric positive definite. `gram_right`: symmetric positive definite.
All inputs are finite; a program needn't handle non-finite values.
Results may differ from a plain program's by a relative error of at most 0.025.
Values may be sent and summed in bfloat16 or wider, within the bound.
A program may use at most 192 MiB of HBM per device.

v0:
```python
import math

import jax
import jax.numpy as jnp
from jax import lax
from jax.experimental import pallas as pl
from jax.experimental.pallas import tpu as pltpu
from jax.sharding import PartitionSpec as P

BLK = 512
MESH = pl.DeviceIdType.MESH
VMEM_LIMIT = 60 * 1024 * 1024

norm_epsilon = 1e-05
decay_rate = 0.9
ridge_shift = 0.001


def meet(devices):
    barrier = pltpu.get_barrier_semaphore()
    for device in devices:
        pl.semaphore_signal(barrier, inc=1, device_id=device, device_id_type=MESH)
    pl.semaphore_wait(barrier, len(devices))


def exchange(collective_id, srcs, out_lead, drop_lead, plan):
    count = len(srcs)
    with_keep = plan.keeps
    copy_total = plan.copies * count

    def kernel(*refs):
        ins, outs = refs[:count], refs[count : 2 * count]
        send_sem, recv_sem, keep_sem = refs[2 * count :]
        items, keep = plan()
        meet([device for _, _, device in items])
        copies = []
        for item_no, (src_index, dst_index, device) in enumerate(items):
            for part_no in range(count):
                at = item_no * count + part_no
                copy = pltpu.make_async_remote_copy(
                    src_ref=ins[part_no].at[src_index],
                    dst_ref=outs[part_no].at[dst_index],
                    send_sem=send_sem.at[at],
                    recv_sem=recv_sem.at[at],
                    device_id=device,
                    device_id_type=MESH,
                )
                copy.start()
                copies.append(copy)
        kept = []
        if with_keep:
            for part_no in range(count):
                copy = pltpu.make_async_copy(
                    ins[part_no].at[keep[0]], outs[part_no].at[keep[1]], keep_sem.at[part_no]
                )
                copy.start()
                kept.append(copy)
        for copy in kept + copies:
            copy.wait()

    return pl.pallas_call(
        kernel,
        out_shape=[
            jax.ShapeDtypeStruct(out_lead + src.shape[drop_lead:], src.dtype) for src in srcs
        ],
        in_specs=[pl.BlockSpec(memory_space=pltpu.VMEM)] * count,
        out_specs=[pl.BlockSpec(memory_space=pl.ANY)] * count,
        scratch_shapes=[
            pltpu.SemaphoreType.DMA((copy_total,)),
            pltpu.SemaphoreType.DMA((copy_total,)),
            pltpu.SemaphoreType.DMA((count,)),
        ],
        compiler_params=pltpu.CompilerParams(
            collective_id=collective_id, has_side_effects=True, vmem_limit_bytes=VMEM_LIMIT
        ),
    )(*srcs)


class Plan:
    def __init__(self, copies, keeps, build):
        self.copies, self.keeps, self.build = copies, keeps, build

    def __call__(self):
        return self.build()


def swap_slots(collective_id, srcs, axis):
    size = lax.axis_size(axis)

    def build():
        me = lax.axis_index(axis)
        items = []
        for step in range(1, size):
            other = lax.rem(me + step, size)
            items.append(((other,), (me,), {axis: other}))
        return items, ((me,), (me,))

    return exchange(collective_id, srcs, (size,), 1, Plan(size - 1, True, build))


def scatter_slots(collective_id, srcs, axis, stride=1):
    size = lax.axis_size(axis) // stride

    def build():
        position = lax.axis_index(axis)
        me, rest = position // stride, lax.rem(position, stride)
        items = []
        for step in range(1, size):
            other = lax.rem(me + step, size)
            items.append(((other,), (step - 1,), {axis: other * stride + rest}))
        return items, None

    return exchange(collective_id, srcs, (size - 1,), 1, Plan(size - 1, False, build))


def pair_half(collective_id, srcs):
    chips = lax.axis_size("dp") // 2

    def build():
        me = lax.axis_index("dp")
        core = lax.rem(me, 2)
        other = 1 - core
        return [((slice(None), other), (slice(None),), {"dp": me - core + other})], None

    return exchange(collective_id, srcs, (chips,), 2, Plan(1, False, build))


def gather_across(collective_id, srcs):
    size = lax.axis_size("mp")

    def build():
        me = lax.axis_index("mp")
        far = 1 - lax.axis_index("section")
        items = []
        for step in range(size):
            other = lax.rem(me + step, size)
            items.append(((0,), (me,), {"section": far, "mp": other}))
        return items, None

    return exchange(
        collective_id, [src[None] for src in srcs], (size,), 1, Plan(size, False, build)
    )


def gather_dp(collective_id, srcs):
    count = len(srcs)
    chips = lax.axis_size("dp") // 2

    def kernel(*refs):
        ins, outs = refs[:count], refs[count : 2 * count]
        send_sem, recv_sem, pair_send, pair_recv, keep_sem = refs[2 * count :]
        position = lax.axis_index("dp")
        chip, core = position // 2, lax.rem(position, 2)
        partner = chip * 2 + 1 - core
        others = [lax.rem(chip + step, chips) for step in range(1, chips)]
        meet([{"dp": partner}] + [{"dp": other * 2 + core} for other in others])
        away, handed, kept = [], [], []
        for step, other in enumerate(others):
            for part_no in range(count):
                at = step * count + part_no
                copy = pltpu.make_async_remote_copy(
                    src_ref=ins[part_no],
                    dst_ref=outs[part_no].at[chip, core],
                    send_sem=send_sem.at[at],
                    recv_sem=recv_sem.at[at],
                    device_id={"dp": other * 2 + core},
                    device_id_type=MESH,
                )
                copy.start()
                away.append(copy)
        for part_no in range(count):
            copy = pltpu.make_async_remote_copy(
                src_ref=ins[part_no],
                dst_ref=outs[part_no].at[chip, core],
                send_sem=pair_send.at[part_no],
                recv_sem=pair_recv.at[part_no],
                device_id={"dp": partner},
                device_id_type=MESH,
            )
            copy.start()
            handed.append(copy)
            copy = pltpu.make_async_copy(
                ins[part_no], outs[part_no].at[chip, core], keep_sem.at[part_no]
            )
            copy.start()
            kept.append(copy)
        for step in range(1, chips):
            source = lax.rem(chip + chips - step, chips)
            for part_no in range(count):
                away[(step - 1) * count + part_no].wait_recv()
                at = step * count + part_no
                copy = pltpu.make_async_remote_copy(
                    src_ref=outs[part_no].at[source, core],
                    dst_ref=outs[part_no].at[source, core],
                    send_sem=pair_send.at[at],
                    recv_sem=pair_recv.at[at],
                    device_id={"dp": partner},
                    device_id_type=MESH,
                )
                copy.start()
                handed.append(copy)
        for copy in away:
            copy.wait_send()
        for copy in handed + kept:
            copy.wait()

    return pl.pallas_call(
        kernel,
        out_shape=[jax.ShapeDtypeStruct((chips, 2) + src.shape, src.dtype) for src in srcs],
        in_specs=[pl.BlockSpec(memory_space=pltpu.VMEM)] * count,
        out_specs=[pl.BlockSpec(memory_space=pl.ANY)] * count,
        scratch_shapes=[
            pltpu.SemaphoreType.DMA(((chips - 1) * count,)),
            pltpu.SemaphoreType.DMA(((chips - 1) * count,)),
            pltpu.SemaphoreType.DMA((chips * count,)),
            pltpu.SemaphoreType.DMA((chips * count,)),
            pltpu.SemaphoreType.DMA((count,)),
        ],
        compiler_params=pltpu.CompilerParams(
            collective_id=collective_id, has_side_effects=True, vmem_limit_bytes=VMEM_LIMIT
        ),
    )(*srcs)


def reduce_dp(first_id, product, row_sums):
    total, rows, columns = product.shape
    chips = total // 2
    position = lax.axis_index("dp")
    chip, core = position // 2, position % 2
    parts = [
        product.reshape(chips, 2, rows, columns),
        jnp.broadcast_to(row_sums[:, None, :], (total, 8, rows)).reshape(chips, 2, 8, rows),
    ]
    received = pair_half(first_id, parts)
    halves = [
        (
            lax.dynamic_index_in_dim(part, core, 1, keepdims=False).astype(jnp.float32)
            + other.astype(jnp.float32)
        ).astype(part.dtype)
        for part, other in zip(parts, received)
    ]
    received = scatter_slots(first_id + 1, halves, "dp", 2)
    summed = [
        lax.dynamic_index_in_dim(half, chip, 0, keepdims=False).astype(jnp.float32)
        + jnp.sum(other.astype(jnp.float32), axis=0)
        for half, other in zip(halves, received)
    ]
    return summed[0], summed[1][0]


def reduce_mp(collective_id, srcs):
    me = lax.axis_index("mp")
    received = scatter_slots(collective_id, srcs, "mp")
    return [
        lax.dynamic_index_in_dim(src, me, 0, keepdims=False).astype(jnp.float32)
        + jnp.sum(other.astype(jnp.float32), axis=0)
        for src, other in zip(srcs, received)
    ]


def silu_slope(pre_act):
    sigmoid_values = jax.nn.sigmoid(pre_act)
    return sigmoid_values * (1.0 + pre_act * (1.0 - sigmoid_values))


def matmul(left, right, left_dim=1, right_dim=0):
    return lax.dot_general(
        left, right, (((left_dim,), (right_dim,)), ((), ())), preferred_element_type=jnp.float32
    )


def inverse_root(matrix):
    low = jnp.bfloat16
    order = matrix.shape[-1]
    on_diagonal = lax.broadcasted_iota(jnp.int32, (order, order), 0) == lax.broadcasted_iota(
        jnp.int32, (order, order), 1
    )
    identity = jnp.where(on_diagonal, 1.0, 0.0).astype(jnp.float32)
    shifted = matrix + ridge_shift * identity
    norm_sq = jnp.sum(jnp.sum(shifted * shifted, axis=1, keepdims=True), axis=0, keepdims=True)
    factor = 2.5 / jnp.sqrt(norm_sq)
    moment = factor * shifted
    moment_low = moment.astype(low)
    moment_sq = matmul(moment_low, moment_low)
    square = (1.5625 * identity - 0.625 * moment + 0.0625 * moment_sq).astype(low)
    stepped = (1.25 * moment - 0.25 * moment_sq).astype(low)
    third = matmul(square, stepped).astype(low)
    fifth = matmul(square, third)
    scale = jnp.sqrt(jnp.sqrt(factor))
    return scale * (1.5625 * identity - 0.3125 * moment - 0.25 * fifth)


def precondition(block_row, block_col, due, hidden, grads, gram_l, gram_r, root_l, root_r):
    slots = gram_l.shape[0]
    tokens = hidden.shape[0]
    width = grads.shape[2]
    scale = 1.0 / math.sqrt(tokens)

    def kernel(
        row_ref, col_ref, due_ref, hid_ref, grad_ref, gl_ref, gr_ref, rl_ref, rr_ref,
        gl_out, gr_out, rl_out, rr_out, up_out,
    ):
        slot = pl.program_id(0)
        pieces = [grad_ref[piece] for piece in range(grad_ref.shape[0])]
        dy = pieces[0] if len(pieces) == 1 else jnp.concatenate(pieces, axis=1)
        grad_low = (matmul(hid_ref[...], dy, 0, 0) * scale).astype(jnp.bfloat16)
        gl_out[0] = decay_rate * gl_ref[0] + matmul(grad_low, grad_low, 1, 1) * (1.0 / BLK)
        gr_out[0] = decay_rate * gr_ref[0] + matmul(grad_low, grad_low, 0, 0) * (1.0 / BLK)

        @pl.when(due_ref[slot] != 0)
        def _():
            rl_out[0] = inverse_root(gl_out[0]).astype(jnp.bfloat16)
            rr_out[0] = inverse_root(gr_out[0]).astype(jnp.bfloat16)

        @pl.when(due_ref[slot] == 0)
        def _():
            rl_out[0] = rl_ref[0]
            rr_out[0] = rr_ref[0]

        right_part = matmul(grad_low, rr_out[0]).astype(jnp.bfloat16)
        up_out[0] = matmul(rl_out[0], right_part).astype(jnp.bfloat16)

    if width >= BLK:
        per = width // BLK
        grad_spec = pl.BlockSpec(
            (1, tokens, BLK),
            lambda s, row, col, due: (lax.div(col[s], per), 0, lax.rem(col[s], per)),
        )
    else:
        grad_spec = pl.BlockSpec(
            (BLK // width, tokens, width), lambda s, row, col, due: (col[s], 0, 0)
        )
    square_spec = pl.BlockSpec((1, BLK, BLK), lambda s, row, col, due: (s, 0, 0))
    return pl.pallas_call(
        kernel,
        grid_spec=pltpu.PrefetchScalarGridSpec(
            num_scalar_prefetch=3,
            grid=(slots,),
            in_specs=[
                pl.BlockSpec((tokens, BLK), lambda s, row, col, due: (0, row[s])),
                grad_spec,
            ]
            + [square_spec] * 4,
            out_specs=[square_spec] * 5,
        ),
        out_shape=[
            jax.ShapeDtypeStruct(gram_l.shape, jnp.float32),
            jax.ShapeDtypeStruct(gram_l.shape, jnp.float32),
            jax.ShapeDtypeStruct(gram_l.shape, jnp.bfloat16),
            jax.ShapeDtypeStruct(gram_l.shape, jnp.bfloat16),
            jax.ShapeDtypeStruct(gram_l.shape, jnp.bfloat16),
        ],
        compiler_params=pltpu.CompilerParams(
            dimension_semantics=("arbitrary",), vmem_limit_bytes=VMEM_LIMIT
        ),
    )(block_row, block_col, due, hidden, grads, gram_l, gram_r, root_l, root_r)


def on_device(
    activations,
    cotangent,
    norm_gain,
    w_up,
    w_down,
    gram_left,
    gram_right,
    root_left,
    root_right,
    owner_slot,
    eighth,
    refresh_phase,
):
    low, f32 = jnp.bfloat16, jnp.float32
    section_no = lax.axis_index("section")
    dp_no = lax.axis_index("dp")
    mp_no = lax.axis_index("mp")
    dp_count = lax.axis_size("dp")
    mp_count = lax.axis_size("mp")
    micro_count, row_count, model_width = activations.shape
    rows = micro_count * row_count
    tokens = rows * dp_count
    up, down = w_up[0], w_down[0]
    width, shard_ff = up.shape
    is_first = section_no == 0
    gain = lax.dynamic_slice_in_dim(norm_gain[0], dp_no * width, width)

    block_cols = model_width // BLK
    block_rows = shard_ff // BLK
    group = block_rows * block_cols
    per_dev = gram_left.shape[1]
    pick = lambda table: lax.dynamic_slice_in_dim(
        lax.dynamic_index_in_dim(table, section_no, 0, keepdims=False), mp_no * block_rows, block_rows, 0
    ).reshape(-1)
    slots = (dp_no * mp_count + mp_no) * per_dev + jnp.arange(per_dev, dtype=jnp.int32)
    owned = pick(owner_slot)[None, :] == slots[:, None]
    block = jnp.sum(jnp.where(owned, jnp.arange(group, dtype=jnp.int32)[None, :], 0), axis=1)
    is_due = pick(eighth) == refresh_phase[0] % 8
    due = jnp.sum(jnp.where(owned & is_due[None, :], 1, 0), axis=1).astype(jnp.int32)

    mine = jnp.where(is_first, activations, cotangent).reshape(rows, dp_count, width)
    (start,) = swap_slots(0, [mine.transpose(1, 0, 2)], "dp")
    start_flat = start.reshape(tokens, width)

    def gained(flat):
        return (flat.astype(f32) * gain).astype(low)

    def row_squares(flat):
        values = flat.astype(f32)
        return jnp.sum(values * values, axis=-1).reshape(dp_count, rows)

    product = lax.cond(
        is_first,
        lambda: matmul(gained(start_flat), up).astype(low),
        lambda: matmul(start_flat, down).astype(low),
    )
    summed_a, squares = reduce_dp(
        1, product.reshape(dp_count, rows, shard_ff), row_squares(start_flat)
    )
    inverse_rms = lax.rsqrt(squares / model_width + norm_epsilon)
    hidden = jax.nn.silu(summed_a * inverse_rms[:, None]).astype(low)
    (hidden_a,) = gather_dp(3, [hidden])
    hidden_a = hidden_a.reshape(tokens, shard_ff)
    branch = matmul(hidden_a, down, 1, 1).astype(low)
    share = tokens // mp_count
    (branch,) = reduce_mp(4, [branch.reshape(mp_count, share, width)])
    own_rows = lambda flat: lax.dynamic_slice_in_dim(flat, mp_no * share, share, 0)
    start_own = own_rows(start_flat).astype(f32)
    output = (start_own + branch).astype(low)
    (relayed,) = gather_across(5, [output])
    relayed = relayed.reshape(tokens, width)

    product = matmul(gained(relayed), up).astype(low)
    summed_b, squares = reduce_dp(
        6, product.reshape(dp_count, rows, shard_ff), row_squares(relayed)
    )
    inverse_rms = lax.rsqrt(squares / model_width + norm_epsilon)
    pre_act = summed_b * inverse_rms[:, None]
    hidden = jax.nn.silu(pre_act).astype(low)
    grad_pre = (summed_a * silu_slope(pre_act)).astype(low)
    row_dot = jnp.sum(summed_b * grad_pre.astype(f32), axis=-1)
    side = jnp.concatenate(
        [
            jnp.broadcast_to(inverse_rms[None], (8, rows)),
            jnp.broadcast_to(row_dot[None], (8, rows)),
        ]
    )
    grad_pre, hidden_b, side = gather_dp(8, [grad_pre, hidden, side])
    inverse_rms = side[:, :, 0].reshape(tokens)
    row_dot = side[:, :, 8].reshape(mp_count, share)
    grad_normed = matmul(grad_pre.reshape(tokens, shard_ff), up, 1, 1).astype(low)
    grad_normed, row_dot = reduce_mp(
        9,
        [
            grad_normed.reshape(mp_count, share, width),
            jnp.broadcast_to(row_dot[:, None], (mp_count, 8, share)),
        ],
    )
    row_dot = row_dot[0][:, None]
    inverse_rms = own_rows(inverse_rms)[:, None]
    values = own_rows(relayed).astype(f32)
    grad_values = inverse_rms * (
        gain * grad_normed - values * (inverse_rms * inverse_rms * row_dot / model_width)
    )
    grad_input = (start_own + grad_values).astype(low)
    (grad_relayed,) = gather_across(10, [grad_input])
    grad_out = jnp.where(is_first, grad_relayed.reshape(tokens, width), start_flat)
    (grads,) = gather_dp(11, [grad_out])
    hidden_all = jnp.where(is_first, hidden_a, hidden_b.reshape(tokens, shard_ff))

    results = precondition(
        block // block_cols,
        block % block_cols,
        due,
        hidden_all,
        grads.reshape(dp_count, tokens, width),
        gram_left[0],
        gram_right[0],
        root_left[0],
        root_right[0],
    )
    return tuple(result[None] for result in results)


def solution(mesh):
    return jax.shard_map(
        on_device,
        mesh=mesh,
        in_specs=(
            P(None, "dp", None),
            P(None, "dp", None),
            P("section", None),
            P("section", "dp", "mp"),
            P("section", "dp", "mp"),
            P("section", ("dp", "mp"), None, None),
            P("section", ("dp", "mp"), None, None),
            P("section", ("dp", "mp"), None, None),
            P("section", ("dp", "mp"), None, None),
            P(),
            P(),
            P(),
        ),
        out_specs=(
            P("section", ("dp", "mp"), None, None),
            P("section", ("dp", "mp"), None, None),
            P("section", ("dp", "mp"), None, None),
            P("section", ("dp", "mp"), None, None),
            P("section", ("dp", "mp"), None, None),
        ),
        check_vma=False,
    )
```

profile of v0, /device:TPU:0, one launch (start us, length us, event | category | flops | bytes accessed | tf_op | source)
XLA Modules:
  0.0 334.4 jit_solution(4382815326832729506)
XLA Ops:
  0.6 0.0 copy-start
  1.4 0.8 dynamic-slice_compare_fusion
  2.1 0.1 copy.27
  2.2 0.1 eq.43
  2.3 0.8 constant_dynamic-slice_fusion.4
  3.1 0.1 copy.26
  3.2 0.1 eq.37
  3.2 0.8 select_reduce_fusion
  4.0 0.6 and_select_fusion
  4.6 0.0 copy-done
  4.6 1.3 broadcast_select_fusion
  5.9 0.8 reshape.151
  6.7 1.3 copy.34
  8.0 16.0 %shard_map.155 = bf16[4,128,1024]{2,1,0:T(8,128)(2,1)S(1)} custom-call(bf16[4,128,1024]{2,1,0:T(8,128)(2,1)} %bitcast.117), custom_call_target="tpu_custom_call" | custom-call | tf_op jit(solution)/shard_map/pallas_call | solution.py:61
  24.0 0.3 multiply_reduce_fusion
  24.3 0.6 broadcast_in_dim.89.refs_1_
  24.9 4.7 %conditional.1 = (bf16[2,2,128,2048]{3,2,1,0:T(8,128)(2,1)S(1)}) conditional(s32[]{:T(128)} %convert_element_type.120, (bf16[512,1024]{1,0:T(8,128)(2,1)S(1)}, bf16[1024,2048]{1,0:T(8,128)(2,1)}) %tuple.31, (bf16[512,1024]{1,0:T(8,128)(2,1)S(1)}, f32[1024]{0:T(1024)S(1)}, bf16[1024,2048]{1,0:T(8,128)(2,1)}) %tuple.32), branch_computations={%region_2.3_spmd, %region_3.4_spmd} | conditional | flops 2150105088 | bytes 7344136 | solution.py:411
  24.9 4.5 %convolution_convert_fusion.1 = bf16[512,2048]{1,0:T(8,128)(2,1)S(1)} fusion(bf16[1024,2048]{1,0:T(8,128)(2,1)} %get-tuple-element.18, bf16[512,1024]{1,0:T(8,128)(2,1)S(1)} %get-tuple-element.16, f32[1024]{0:T(1024)S(1)} %get-tuple-element.17), kind=kOutput, calls=%fused_computation.1 | convolution fusion | flops 2150105088 | bytes 7344128 | tf_op jit(solution)/shard_map/cond/branch_1_fun/dot_general | solution.py:267
  29.6 3.9 %shard_map.156 = (bf16[2,128,2048]{2,1,0:T(8,128)(2,1)}, f32[2,8,128]{2,1,0:T(8,128)}) custom-call(bf16[2,2,128,2048]{3,2,1,0:T(8,128)(2,1)S(1)} %get-tuple-element.73.refs_0_, f32[2,2,8,128]{3,2,1,0:T(8,128)} %broadcast_in_dim.89.refs_1_), custom_call_target="tpu_custom_call" | custom-call | tf_op jit(solution)/shard_map/pallas_call | solution.py:61
  33.5 0.0 copy-start.5
  33.6 2.6 fusion.4.refs_0_
  36.1 0.0 copy-done.5
  36.1 0.6 broadcast_add_fusion.1.refs_1_
  36.7 15.7 %shard_map.157 = (bf16[1,128,2048]{2,1,0:T(8,128)(2,1)}, f32[1,8,128]{2,1,0:T(8,128)}) custom-call(bf16[2,128,2048]{2,1,0:T(8,128)(2,1)} %fusion.4.refs_0_, f32[2,8,128]{2,1,0:T(8,128)} %broadcast_add_fusion.1.refs_1_), custom_call_target="tpu_custom_call" | custom-call | tf_op jit(solution)/shard_map/pallas_call | solution.py:61
  52.4 0.7 dynamic-slice_add_fusion.1
  53.1 2.4 multiply_convert_fusion.3.refs_0_
  55.5 17.3 %shard_map.158 = bf16[2,2,128,2048]{3,2,1,0:T(8,128)(2,1)} custom-call(bf16[128,2048]{1,0:T(8,128)(2,1)} %multiply_convert_fusion.3.refs_0_), custom_call_target="tpu_custom_call" | custom-call | tf_op jit(solution)/shard_map/pallas_call | solution.py:207
  72.9 6.2 %convolution_convert_fusion.4 = bf16[512,1024]{1,0:T(8,128)(2,1)} fusion(bf16[512,2048]{1,0:T(8,128)(2,1)} %bitcast.109, bf16[1,1024,2048]{2,1,0:T(8,128)(2,1)} %param.18), kind=kOutput, calls=%fused_computation.18 | convolution fusion | flops 2148007936 | bytes 7340032 | tf_op jit(solution)/shard_map/dot_general | solution.py:267
  79.0 23.3 %shard_map.159 = bf16[3,128,1024]{2,1,0:T(8,128)(2,1)} custom-call(bf16[4,128,1024]{2,1,0:T(8,128)(2,1)} %bitcast.118), custom_call_target="tpu_custom_call" | custom-call | tf_op jit(solution)/shard_map/pallas_call | solution.py:61
  102.4 1.3 convert_reduce_fusion.1
  103.7 1.8 fusion.13.refs_0_
  105.4 33.2 %shard_map.160 = bf16[4,128,1024]{2,1,0:T(8,128)(2,1)} custom-call(bf16[1,128,1024]{2,1,0:T(8,128)(2,1)} %fusion.13.refs_0_), custom_call_target="tpu_custom_call" | custom-call | tf_op jit(solution)/shard_map/pallas_call | solution.py:61
  138.6 1.6 fusion.2
  140.2 0.6 broadcast_in_dim.92.refs_1_
  140.8 5.9 %convolution_convert_fusion.2 = bf16[512,2048]{1,0:T(8,128)(2,1)} fusion(bf16[512,1024]{1,0:T(8,128)(2,1)S(1)} %bitcast.122, bf16[1,1024,2048]{2,1,0:T(8,128)(2,1)} %param.17), kind=kOutput, calls=%fused_computation.4 | convolution fusion | flops 2148532224 | bytes 7340032 | tf_op jit(solution)/shard_map/dot_general | solution.py:267
  146.7 4.4 %shard_map.161 = (bf16[2,128,2048]{2,1,0:T(8,128)(2,1)}, f32[2,8,128]{2,1,0:T(8,128)}) custom-call(bf16[2,2,128,2048]{3,2,1,0:T(8,128)(2,1)} %bitcast.111, f32[2,2,8,128]{3,2,1,0:T(8,128)} %broadcast_in_dim.92.refs_1_), custom_call_target="tpu_custom_call" | custom-call | tf_op jit(solution)/shard_map/pallas_call | solution.py:61
  151.2 0.0 copy-start.4
  151.2 0.0 copy-start.2
  151.2 0.0 copy-start.3
  151.2 3.0 fusion.3.refs_0_
  154.2 0.6 broadcast_add_fusion.refs_1_
  154.8 15.4 %shard_map.162 = (bf16[1,128,2048]{2,1,0:T(8,128)(2,1)}, f32[1,8,128]{2,1,0:T(8,128)}) custom-call(bf16[2,128,2048]{2,1,0:T(8,128)(2,1)} %fusion.3.refs_0_, f32[2,8,128]{2,1,0:T(8,128)} %broadcast_add_fusion.refs_1_), custom_call_target="tpu_custom_call" | custom-call | tf_op jit(solution)/shard_map/pallas_call | solution.py:61
  170.3 0.7 dynamic-slice_add_fusion
  171.0 0.0 copy-done.3
  171.0 3.0 fusion.5
  174.0 0.6 pad_maximum_fusion.refs_2_
  174.6 28.0 %shard_map.163 = (bf16[2,2,128,2048]{3,2,1,0:T(8,128)(2,1)}, bf16[2,2,128,2048]{3,2,1,0:T(8,128)(2,1)}, f32[2,2,16,128]{3,2,1,0:T(8,128)}) custom-call(bf16[128,2048]{1,0:T(8,128)(2,1)} %get-tuple-element.65.refs_0_, bf16[128,2048]{1,0:T(8,128)(2,1)} %get-tuple-element.66.refs_1_, f32[16,128]{1,0:T(8,128)} %pad_maximum_fusion.refs_2_), custom_call_target="tpu_custom_call" | custom-call | tf_op jit(solution)/shard_map/pallas_call | solution.py:207
  202.7 0.0 copy-start.6
  202.7 0.0 copy-start.7
  202.7 3.9 %bitcast_select_fusion.hid_ref = bf16[512,2048]{1,0:T(8,128)(2,1)} fusion(bf16[2,2,128,2048]{3,2,1,0:T(8,128)(2,1)} %get-tuple-element.50, pred[]{:T(512)S(6)} %eq.44, bf16[2,2,128,2048]{3,2,1,0:T(8,128)(2,1)} %shard_map.158), kind=kLoop, calls=%fused_computation.13 | loop fusion | flops 1048576 | bytes 6291457 | tf_op jit(solution)/shard_map/jit(_where)/select_n | solution.py:468
  206.6 0.7 fusion.21
  207.3 0.6 broadcast_in_dim.96.refs_1_
  208.0 0.0 copy-done.6
  208.0 3.3 convolution_convert_fusion.3
  211.3 23.1 %shard_map.164 = (bf16[3,128,1024]{2,1,0:T(8,128)(2,1)}, f32[3,8,128]{2,1,0:T(8,128)}) custom-call(bf16[4,128,1024]{2,1,0:T(8,128)(2,1)} %bitcast.120, f32[4,8,128]{2,1,0:T(8,128)} %broadcast_in_dim.96.refs_1_), custom_call_target="tpu_custom_call" | custom-call | tf_op jit(solution)/shard_map/pallas_call | solution.py:61
  234.4 1.3 convert_reduce_fusion
  235.7 0.7 reduce_sum.83
  236.5 0.1 fusion.16
  236.5 2.0 fusion.12.refs_0_
  238.5 32.6 %shard_map.165 = bf16[4,128,1024]{2,1,0:T(8,128)(2,1)} custom-call(bf16[1,128,1024]{2,1,0:T(8,128)(2,1)} %fusion.12.refs_0_), custom_call_target="tpu_custom_call" | custom-call | tf_op jit(solution)/shard_map/pallas_call | solution.py:61
  271.1 2.3 bitcast_select_fusion.1.refs_0_
  273.4 29.2 %shard_map.166 = bf16[2,2,512,1024]{3,2,1,0:T(8,128)(2,1)} custom-call(bf16[512,1024]{1,0:T(8,128)(2,1)} %bitcast_select_fusion.1.refs_0_), custom_call_target="tpu_custom_call" | custom-call | tf_op jit(solution)/shard_map/pallas_call | solution.py:207
  302.6 0.0 copy-start.1
  302.6 31.7 %shard_map.167 = (f32[8,512,512]{2,1,0:T(8,128)}, f32[8,512,512]{2,1,0:T(8,128)}, bf16[8,512,512]{2,1,0:T(8,128)(2,1)}, bf16[8,512,512]{2,1,0:T(8,128)(2,1)}, bf16[8,512,512]{2,1,0:T(8,128)(2,1)}) custom-call(s32[8]{0:T(128)} %get-tuple-element.72.row_ref, s32[8]{0:T(128)} %get-tuple-element.71.col_ref, s32[8]{0:T(128)} %get-tuple-element.60.due_ref, ...), custom_call_target="tpu_custom_call" | custom-call | tf_op jit(solution)/shard_map/pallas_call | solution.py:334
  (14 shorter events, 0.1 us)
Async XLA Ops:
  0.6 4.0 %copy-start = (f32[1,4096]{1,0:T(1,128)S(1)}, f32[1,4096]{1,0:T(1,128)}, u32[]{:S(2)}) copy-start(f32[1,4096]{1,0:T(1,128)} %param.16) | copy-start | bytes 49156
  33.5 2.6 copy-start.5
  151.2 3.1 copy-start.4
  151.2 19.8 %copy-start.2 = (bf16[2,128,2048]{2,1,0:T(8,128)(2,1)S(1)}, bf16[2,128,2048]{2,1,0:T(8,128)(2,1)}, u32[]{:S(2)}) copy-start(bf16[2,128,2048]{2,1,0:T(8,128)(2,1)} %fusion.4.refs_0_) | copy-start | bytes 3145732
  151.2 19.8 %copy-start.3 = (bf16[1,128,2048]{2,1,0:T(8,128)(2,1)S(1)}, bf16[1,128,2048]{2,1,0:T(8,128)(2,1)}, u32[]{:S(2)}) copy-start(bf16[1,128,2048]{2,1,0:T(8,128)(2,1)} %get-tuple-element.44) | copy-start | bytes 1572868
  202.7 5.3 %copy-start.6 = (bf16[1,1024,2048]{2,1,0:T(8,128)(2,1)S(1)}, bf16[1,1024,2048]{2,1,0:T(8,128)(2,1)}, u32[]{:S(2)}) copy-start(bf16[1,1024,2048]{2,1,0:T(8,128)(2,1)} %param.17) | copy-start | bytes 12582916
  202.7 5.3 %copy-start.7 = (bf16[2,2,128,2048]{3,2,1,0:T(8,128)(2,1)S(1)}, bf16[2,2,128,2048]{3,2,1,0:T(8,128)(2,1)}, u32[]{:S(2)}) copy-start(bf16[2,2,128,2048]{3,2,1,0:T(8,128)(2,1)} %get-tuple-element.52) | copy-start | bytes 6291460
  302.6 31.7 %copy-start.1 = (f32[1,4096]{1,0:T(1,128)S(1)}, f32[1,4096]{1,0:T(1,128)}, u32[]{:S(2)}) copy-start(f32[1,4096]{1,0:T(1,128)} %param.16) | copy-start | bytes 49156
where the time goes:
time: 335 us; the launch traced here: 334 us
  Pallas kernels  274 us (82%)
  other arithmetic  33 us (10%)
  matrix products  19.9 us (6%)
  local copies, waits for them, and re-layouts  5.84 us (2%)
    pallas_call x9, Pallas kernels, exchange(): pl.pallas_call(kernel, out_shape=[jax.ShapeDtypeStruct(out_lead + src.sha...  168 us
    pallas_call x3, Pallas kernels, gather_dp(): pl.pallas_call(kernel, out_shape=[jax.ShapeDtypeStruct((chips, 2) + src.s...  74.5 us
    pallas_call x1, Pallas kernels, precondition(): pl.pallas_call(kernel, grid_spec=pltpu.PrefetchScalarGridSpec(num_scalar_...  31.7 us
    dot_general x4, matrix products, matmul(): lax.dot_general(left, right, (((left_dim,), (right_dim,)), ((), ())), pre...  19.9 us

commit v1 on v0

--- a/solution.py
+++ b/solution.py
@@ -125,101 +125,255 @@
     return exchange(collective_id, srcs, (chips,), 2, Plan(1, False, build))
 
 
-def gather_across(collective_id, srcs):
-    size = lax.axis_size("mp")
-
-    def build():
-        me = lax.axis_index("mp")
-        far = 1 - lax.axis_index("section")
-        items = []
-        for step in range(size):
-            other = lax.rem(me + step, size)
-            items.append(((0,), (me,), {"section": far, "mp": other}))
-        return items, None
-
-    return exchange(
-        collective_id, [src[None] for src in srcs], (size,), 1, Plan(size, False, build)
+def gather_parts(refs_in, refs_out, sems):
+    away_send, away_recv, pair_send, pair_recv, keep_sem = sems
+    chips = lax.axis_size("dp") // 2
+    position = lax.axis_index("dp")
+    chip, core = position // 2, lax.rem(position, 2)
+    partner = {"dp": chip * 2 + 1 - core}
+    others = [lax.rem(chip + step, chips) for step in range(1, chips)]
+    parts = []
+    for ref_in, ref_out in zip(refs_in, refs_out):
+        pieces = pieces_of(ref_in.shape[0])
+        for piece in range(pieces):
+            size = ref_in.shape[0] // pieces
+            parts.append((ref_in, ref_out, pl.ds(piece * size, size)))
+    count = len(parts)
+
+    def away_copy(step, part_no):
+        ref_in, ref_out, window = parts[part_no]
+        at = (step - 1) * count + part_no
+        return pltpu.make_async_remote_copy(
+            src_ref=ref_in.at[window],
+            dst_ref=ref_out.at[chip, core, window],
+            send_sem=away_send.at[at],
+            recv_sem=away_recv.at[at],
+            device_id={"dp": others[step - 1] * 2 + core},
+            device_id_type=MESH,
+        )
+
+    def pair_copy(step, part_no):
+        ref_in, ref_out, window = parts[part_no]
+        source = lax.rem(chip + chips - step, chips)
+        at = step * count + part_no
+        return pltpu.make_async_remote_copy(
+            src_ref=ref_in.at[window] if step == 0 else ref_out.at[source, core, window],
+            dst_ref=ref_out.at[source, core, window],
+            send_sem=pair_send.at[at],
+            recv_sem=pair_recv.at[at],
+            device_id=partner,
+            device_id_type=MESH,
+        )
+
+    def keep_copy(part_no):
+        ref_in, ref_out, window = parts[part_no]
+        return pltpu.make_async_copy(
+            ref_in.at[window], ref_out.at[chip, core, window], keep_sem.at[part_no]
+        )
+
+    def begin():
+        for part_no in range(count):
+            for step in range(1, chips):
+                away_copy(step, part_no).start()
+        for part_no in range(count):
+            pair_copy(0, part_no).start()
+            keep_copy(part_no).start()
+
+    def finish():
+        for part_no in range(count):
+            for step in range(1, chips):
+                away_copy(step, part_no).wait_recv()
+                pair_copy(step, part_no).start()
+        for part_no in range(count):
+            keep_copy(part_no).wait()
+            for step in range(1, chips):
+                away_copy(step, part_no).wait_send()
+            for step in range(chips):
+                pair_copy(step, part_no).wait()
+
+    return [partner] + [{"dp": other * 2 + core} for other in others], begin, finish
+
+
+def pieces_of(rows):
+    return 4 if rows % 64 == 0 else 1
+
+
+def gather_shapes(srcs):
+    chips = lax.axis_size("dp") // 2
+    count = sum(pieces_of(src.shape[0]) for src in srcs)
+    dma = pltpu.SemaphoreType.DMA
+    return (
+        [jax.ShapeDtypeStruct((chips, 2) + src.shape, src.dtype) for src in srcs],
+        [
+            dma(((chips - 1) * count,)),
+            dma(((chips - 1) * count,)),
+            dma((chips * count,)),
+            dma((chips * count,)),
+            dma((count,)),
+        ],
     )
 
 
 def gather_dp(collective_id, srcs):
     count = len(srcs)
-    chips = lax.axis_size("dp") // 2
+    shapes, sems = gather_shapes(srcs)
 
     def kernel(*refs):
-        ins, outs = refs[:count], refs[count : 2 * count]
-        send_sem, recv_sem, pair_send, pair_recv, keep_sem = refs[2 * count :]
-        position = lax.axis_index("dp")
-        chip, core = position // 2, lax.rem(position, 2)
-        partner = chip * 2 + 1 - core
-        others = [lax.rem(chip + step, chips) for step in range(1, chips)]
-        meet([{"dp": partner}] + [{"dp": other * 2 + core} for other in others])
-        away, handed, kept = [], [], []
-        for step, other in enumerate(others):
-            for part_no in range(count):
-                at = step * count + part_no
-                copy = pltpu.make_async_remote_copy(
-                    src_ref=ins[part_no],
-                    dst_ref=outs[part_no].at[chip, core],
-                    send_sem=send_sem.at[at],
-                    recv_sem=recv_sem.at[at],
-                    device_id={"dp": other * 2 + core},
-                    device_id_type=MESH,
-                )
-                copy.start()
-                away.append(copy)
-        for part_no in range(count):
-            copy = pltpu.make_async_remote_copy(
-                src_ref=ins[part_no],
-                dst_ref=outs[part_no].at[chip, core],
-                send_sem=pair_send.at[part_no],
-                recv_sem=pair_recv.at[part_no],
-                device_id={"dp": partner},
-                device_id_type=MESH,
-            )
-            copy.start()
-            handed.append(copy)
-            copy = pltpu.make_async_copy(
-                ins[part_no], outs[part_no].at[chip, core], keep_sem.at[part_no]
-            )
-            copy.start()
-            kept.append(copy)
-        for step in range(1, chips):
-            source = lax.rem(chip + chips - step, chips)
-            for part_no in range(count):
-                away[(step - 1) * count + part_no].wait_recv()
-                at = step * count + part_no
-                copy = pltpu.make_async_remote_copy(
-                    src_ref=outs[part_no].at[source, core],
-                    dst_ref=outs[part_no].at[source, core],
-                    send_sem=pair_send.at[at],
-                    recv_sem=pair_recv.at[at],
-                    device_id={"dp": partner},
-                    device_id_type=MESH,
-                )
-                copy.start()
-                handed.append(copy)
-        for copy in away:
-            copy.wait_send()
-        for copy in handed + kept:
-            copy.wait()
+        greet, begin, finish = gather_parts(
+            refs[:count], refs[count : 2 * count], refs[2 * count :]
+        )
+        meet(greet)
+        begin()
+        finish()
 
     return pl.pallas_call(
         kernel,
-        out_shape=[jax.ShapeDtypeStruct((chips, 2) + src.shape, src.dtype) for src in srcs],
+        out_shape=shapes,
         in_specs=[pl.BlockSpec(memory_space=pltpu.VMEM)] * count,
         out_specs=[pl.BlockSpec(memory_space=pl.ANY)] * count,
-        scratch_shapes=[
-            pltpu.SemaphoreType.DMA(((chips - 1) * count,)),
-            pltpu.SemaphoreType.DMA(((chips - 1) * count,)),
-            pltpu.SemaphoreType.DMA((chips * count,)),
-            pltpu.SemaphoreType.DMA((chips * count,)),
-            pltpu.SemaphoreType.DMA((count,)),
-        ],
+        scratch_shapes=sems,
         compiler_params=pltpu.CompilerParams(
             collective_id=collective_id, has_side_effects=True, vmem_limit_bytes=VMEM_LIMIT
         ),
     )(*srcs)
+
+
+def relay(collective_id, sender, product, operands, finish_rows, side=None, aside=None):
+    size, share, width = product.shape
+    pieces = pieces_of(share)
+    rows = share // pieces
+    operand_total = len(operands)
+    has_side, has_aside = side is not None, aside is not None
+    hops = size - 1
+    aside_shapes, aside_sems = gather_shapes([aside]) if has_aside else ([], [])
+
+    def kernel(*refs):
+        refs = list(refs)
+        take = lambda n: [refs.pop(0) for _ in range(n)]
+        (product_ref,) = take(1)
+        operand_refs = take(operand_total)
+        side_ref = take(1)[0] if has_side else None
+        aside_in = take(1) if has_aside else []
+        (out_ref,) = take(1)
+        aside_out = take(1) if has_aside else []
+        landed, ready = take(2)
+        side_landed = take(1)[0] if has_side else None
+        sum_send, sum_recv, far_send, far_recv, side_send, side_recv = take(6)
+        me = lax.axis_index("mp")
+        section = lax.axis_index("section")
+        far = 1 - section
+        ring = [lax.rem(me + step, size) for step in range(size)]
+        greet = [{"mp": ring[step]} for step in range(1, size)]
+        greet += [{"section": far, "mp": other} for other in ring]
+        if has_aside:
+            aside_greet, begin, finish = gather_parts(aside_in, aside_out, refs)
+            greet += aside_greet
+        meet(greet)
+
+        def sum_copy(piece, step):
+            window = pl.ds(piece * rows, rows)
+            at = piece * hops + step - 1
+            return pltpu.make_async_remote_copy(
+                src_ref=product_ref.at[ring[step], window],
+                dst_ref=landed.at[step - 1, window],
+                send_sem=sum_send.at[at],
+                recv_sem=sum_recv.at[at],
+                device_id={"mp": ring[step]},
+                device_id_type=MESH,
+            )
+
+        def side_copy(step):
+            return pltpu.make_async_remote_copy(
+                src_ref=side_ref.at[ring[step]],
+                dst_ref=side_landed.at[step - 1],
+                send_sem=side_send.at[step - 1],
+                recv_sem=side_recv.at[step - 1],
+                device_id={"mp": ring[step]},
+                device_id_type=MESH,
+            )
+
+        def far_copy(piece, step):
+            at = piece * size + step
+            window = pl.ds(piece * rows, rows)
+            return pltpu.make_async_remote_copy(
+                src_ref=ready.at[window],
+                dst_ref=out_ref.at[me, window],
+                send_sem=far_send.at[at],
+                recv_sem=far_recv.at[at],
+                device_id={"section": far, "mp": ring[step]},
+                device_id_type=MESH,
+            )
+
+        @pl.when(section == sender)
+        def _():
+            if has_side:
+                for step in range(1, size):
+                    side_copy(step).start()
+            for piece in range(pieces):
+                for step in range(1, size):
+                    sum_copy(piece, step).start()
+            if has_aside:
+                begin()
+            if has_side:
+                for step in range(1, size):
+                    side_copy(step).wait()
+            for piece in range(pieces):
+                for step in range(1, size):
+                    sum_copy(piece, step).wait_recv()
+                window = pl.ds(piece * rows, rows)
+                total = product_ref[me, window, :].astype(jnp.float32)
+                for step in range(1, size):
+                    total += landed[step - 1, window, :].astype(jnp.float32)
+                side_total = None
+                if has_side:
+                    side_total = side_ref[me, window, :].astype(jnp.float32)
+                    for step in range(1, size):
+                        side_total += side_landed[step - 1, window, :].astype(jnp.float32)
+                cut = [
+                    ref[window, :] if ref.shape[0] == share else ref[...] for ref in operand_refs
+                ]
+                ready[window, :] = finish_rows(total, side_total, *cut).astype(ready.dtype)
+                for step in range(size):
+                    far_copy(piece, step).start()
+            if has_aside:
+                finish()
+            for piece in range(pieces):
+                for step in range(1, size):
+                    sum_copy(piece, step).wait_send()
+                for step in range(size):
+                    far_copy(piece, step).wait_send()
+
+        @pl.when(section != sender)
+        def _():
+            for piece in range(pieces):
+                for step in range(size):
+                    far_copy(piece, step).wait_recv()
+
+    dma = pltpu.SemaphoreType.DMA
+    inputs = [product] + list(operands) + [x for x in (side, aside) if x is not None]
+    return pl.pallas_call(
+        kernel,
+        out_shape=[jax.ShapeDtypeStruct(product.shape, jnp.bfloat16)] + aside_shapes,
+        in_specs=[pl.BlockSpec(memory_space=pltpu.VMEM)] * len(inputs),
+        out_specs=[pl.BlockSpec(memory_space=pl.ANY)] * (1 + len(aside_shapes)),
+        scratch_shapes=[
+            pltpu.VMEM((hops, share, width), product.dtype),
+            pltpu.VMEM((share, width), jnp.bfloat16),
+        ]
+        + ([pltpu.VMEM((hops,) + side.shape[1:], side.dtype)] if has_side else [])
+        + [
+            dma((pieces * hops,)),
+            dma((pieces * hops,)),
+            dma((pieces * size,)),
+            dma((pieces * size,)),
+            dma((hops,)),
+            dma((hops,)),
+        ]
+        + aside_sems,
+        compiler_params=pltpu.CompilerParams(
+            collective_id=collective_id, has_side_effects=True, vmem_limit_bytes=VMEM_LIMIT
+        ),
+    )(*inputs)
 
 
 def reduce_dp(first_id, product, row_sums):
@@ -246,16 +400,6 @@
         for half, other in zip(halves, received)
     ]
     return summed[0], summed[1][0]
-
-
-def reduce_mp(collective_id, srcs):
-    me = lax.axis_index("mp")
-    received = scatter_slots(collective_id, srcs, "mp")
-    return [
-        lax.dynamic_index_in_dim(src, me, 0, keepdims=False).astype(jnp.float32)
-        + jnp.sum(other.astype(jnp.float32), axis=0)
-        for src, other in zip(srcs, received)
-    ]
 
 
 def silu_slope(pre_act):
@@ -422,11 +566,15 @@
     hidden_a = hidden_a.reshape(tokens, shard_ff)
     branch = matmul(hidden_a, down, 1, 1).astype(low)
     share = tokens // mp_count
-    (branch,) = reduce_mp(4, [branch.reshape(mp_count, share, width)])
     own_rows = lambda flat: lax.dynamic_slice_in_dim(flat, mp_no * share, share, 0)
-    start_own = own_rows(start_flat).astype(f32)
-    output = (start_own + branch).astype(low)
-    (relayed,) = gather_across(5, [output])
+    start_own = own_rows(start_flat)
+    (relayed,) = relay(
+        4,
+        0,
+        branch.reshape(mp_count, share, width),
+        [start_own],
+        lambda total, side, base: base.astype(f32) + total,
+    )
     relayed = relayed.reshape(tokens, width)
 
     product = matmul(gained(relayed), up).astype(low)
@@ -444,25 +592,37 @@
             jnp.broadcast_to(row_dot[None], (8, rows)),
         ]
     )
-    grad_pre, hidden_b, side = gather_dp(8, [grad_pre, hidden, side])
-    inverse_rms = side[:, :, 0].reshape(tokens)
-    row_dot = side[:, :, 8].reshape(mp_count, share)
+    grad_pre, side = gather_dp(8, [grad_pre, side])
+    inverse_rms = own_rows(side[:, :, 0].reshape(tokens))[:, None]
+    row_dot = side[:, :, 8].reshape(tokens, 1)
+    dot_high = row_dot.astype(low)
+    dot_low = (row_dot - lax.optimization_barrier(dot_high).astype(f32)).astype(low)
+    dots = jnp.where(jnp.arange(128)[None, :] < 64, dot_high, dot_low)
     grad_normed = matmul(grad_pre.reshape(tokens, shard_ff), up, 1, 1).astype(low)
-    grad_normed, row_dot = reduce_mp(
+    spread = lambda column: jnp.broadcast_to(column, (share, 128))
+
+    def input_gradient(total, side, base, values, rms, cubed, gain_row):
+        row_dot = side[:, 0:1] + side[:, 64:65]
+        return base.astype(f32) + (
+            rms[:, 0:1] * (gain_row * total)
+            - values.astype(f32) * (cubed[:, 0:1] * row_dot)
+        )
+
+    grad_relayed, hidden_b = relay(
         9,
+        1,
+        grad_normed.reshape(mp_count, share, width),
         [
-            grad_normed.reshape(mp_count, share, width),
-            jnp.broadcast_to(row_dot[:, None], (mp_count, 8, share)),
+            start_own,
+            own_rows(relayed),
+            spread(inverse_rms),
+            spread(inverse_rms * inverse_rms * inverse_rms / model_width),
+            gain[None],
         ],
-    )
-    row_dot = row_dot[0][:, None]
-    inverse_rms = own_rows(inverse_rms)[:, None]
-    values = own_rows(relayed).astype(f32)
-    grad_values = inverse_rms * (
-        gain * grad_normed - values * (inverse_rms * inverse_rms * row_dot / model_width)
-    )
-    grad_input = (start_own + grad_values).astype(low)
-    (grad_relayed,) = gather_across(10, [grad_input])
+        input_gradient,
+        side=dots.reshape(mp_count, share, 128),
+        aside=hidden,
+    )
     grad_out = jnp.where(is_first, grad_relayed.reshape(tokens, width), start_flat)
     (grads,) = gather_dp(11, [grad_out])
     hidden_all = jnp.where(is_first, hidden_a, hidden_b.reshape(tokens, shard_ff))

time: 335 us -> 313 us (0.934)
  Pallas kernels: 274 us -> 251 us
  other arithmetic: 33 us -> 25 us
  local copies, waits for them, and re-layouts: 5.84 us -> 9.89 us
    pallas_call x9 -> x5, Pallas kernels: 168 us -> 55.4 us  [exchange(): pl.pallas_call(kernel, out_shape=[jax.ShapeDtypeStruct(out_lead + src.sha...]
    pallas_call x3 -> x5, Pallas kernels: 74.5 us -> 168 us  [the longest x2 107 us: relay(): pl.pallas_call(kernel, out_shape=[jax.ShapeDtypeStruct(product.shape, jnp...]
    pallas_call x1, Pallas kernels: 31.7 us -> 27.2 us  [precondition(): pl.pallas_call(kernel, grid_spec=pltpu.PrefetchScalarGridSpec(num_scalar_...]
    broadcast_in_dim x2 -> x0, other arithmetic: 3.73 us -> none  [gather_across(): src[None]]
where the time goes in v1:
time: 313 us; the launch traced here: 310 us
  Pallas kernels  251 us (80%)
  other arithmetic  25 us (8%)
  matrix products  22.7 us (7%)
  local copies, waits for them, and re-layouts  9.89 us (3%)
    pallas_call x2, Pallas kernels, relay(): pl.pallas_call(kernel, out_shape=[jax.ShapeDtypeStruct(product.shape, jnp...  107 us
    pallas_call x3, Pallas kernels, gather_dp(): pl.pallas_call(kernel, out_shape=shapes, in_specs=[pl.BlockSpec(memory_sp...  61.2 us
    pallas_call x5, Pallas kernels, exchange(): pl.pallas_call(kernel, out_shape=[jax.ShapeDtypeStruct(out_lead + src.sha...  55.4 us
    pallas_call x1, Pallas kernels, precondition(): pl.pallas_call(kernel, grid_spec=pltpu.PrefetchScalarGridSpec(num_scalar_...  27.2 us
    dot_general x4, matrix products, matmul(): lax.dot_general(left, right, (((left_dim,), (right_dim,)), ((), ())), pre...  22.7 us

profile of v1, /device:TPU:0, one launch (start us, length us, event | category | flops | bytes accessed | tf_op | source)
XLA Modules:
  0.0 310.3 jit_solution(17352617234850087939)
XLA Ops:
  0.6 0.0 copy-start
  1.4 0.8 dynamic-slice_compare_fusion
  2.1 0.1 copy.27
  2.2 0.1 eq.43
  2.3 0.8 constant_dynamic-slice_fusion.5
  3.1 0.1 copy.26
  3.2 0.1 eq.37
  3.3 0.8 select_reduce_fusion
  4.0 0.6 and_select_fusion
  4.6 0.0 copy-done
  4.6 1.3 broadcast_select_fusion
  6.0 0.8 reshape.179
  6.8 1.3 copy.35
  8.1 16.0 %shard_map.155 = bf16[4,128,1024]{2,1,0:T(8,128)(2,1)S(1)} custom-call(bf16[4,128,1024]{2,1,0:T(8,128)(2,1)} %bitcast.102), custom_call_target="tpu_custom_call" | custom-call | tf_op jit(solution)/shard_map/pallas_call | solution.py:61
  24.1 0.3 multiply_reduce_fusion
  24.4 0.6 broadcast_in_dim.109.refs_1_
  25.0 0.7 constant_dynamic-slice_fusion.2.refs_1_
  25.7 4.5 %conditional.1 = (bf16[2,2,128,2048]{3,2,1,0:T(8,128)(2,1)S(1)}) conditional(s32[]{:T(128)} %convert_element_type.113, (bf16[512,1024]{1,0:T(8,128)(2,1)S(1)}, bf16[1024,2048]{1,0:T(8,128)(2,1)}) %tuple.31, (bf16[512,1024]{1,0:T(8,128)(2,1)S(1)}, f32[1024]{0:T(1024)S(1)}, bf16[1024,2048]{1,0:T(8,128)(2,1)}) %tuple.32), branch_computations={%region_2.3_spmd, %region_3.4_spmd} | conditional | flops 2150105088 | bytes 7344136 | solution.py:555
  25.7 4.5 %convolution_convert_fusion.1 = bf16[512,2048]{1,0:T(8,128)(2,1)S(1)} fusion(bf16[1024,2048]{1,0:T(8,128)(2,1)} %get-tuple-element.18, bf16[512,1024]{1,0:T(8,128)(2,1)S(1)} %get-tuple-element.16, f32[1024]{0:T(1024)S(1)} %get-tuple-element.17), kind=kOutput, calls=%fused_computation.1 | convolution fusion | flops 2150105088 | bytes 7344128 | tf_op jit(solution)/shard_map/cond/branch_1_fun/dot_general | solution.py:411
  30.2 3.9 %shard_map.156 = (bf16[2,128,2048]{2,1,0:T(8,128)(2,1)}, f32[2,8,128]{2,1,0:T(8,128)}) custom-call(bf16[2,2,128,2048]{3,2,1,0:T(8,128)(2,1)S(1)} %get-tuple-element.71.refs_0_, f32[2,2,8,128]{3,2,1,0:T(8,128)} %broadcast_in_dim.109.refs_1_), custom_call_target="tpu_custom_call" | custom-call | tf_op jit(solution)/shard_map/pallas_call | solution.py:61
  34.1 0.0 copy-start.7
  34.1 2.6 fusion.4.refs_0_
  36.7 0.0 copy-done.7
  36.7 0.6 broadcast_add_fusion.1.refs_1_
  37.3 15.7 %shard_map.157 = (bf16[1,128,2048]{2,1,0:T(8,128)(2,1)}, f32[1,8,128]{2,1,0:T(8,128)}) custom-call(bf16[2,128,2048]{2,1,0:T(8,128)(2,1)} %fusion.4.refs_0_, f32[2,8,128]{2,1,0:T(8,128)} %broadcast_add_fusion.1.refs_1_), custom_call_target="tpu_custom_call" | custom-call | tf_op jit(solution)/shard_map/pallas_call | solution.py:61
  53.0 0.7 dynamic-slice_add_fusion.1
  53.7 2.4 multiply_convert_fusion.3.refs_0_
  56.1 17.0 %shard_map.158 = bf16[2,2,128,2048]{3,2,1,0:T(8,128)(2,1)} custom-call(bf16[128,2048]{1,0:T(8,128)(2,1)} %multiply_convert_fusion.3.refs_0_), custom_call_target="tpu_custom_call" | custom-call | tf_op jit(solution)/shard_map/pallas_call | solution.py:229
  73.1 6.2 %convolution_convert_fusion.4 = bf16[512,1024]{1,0:T(8,128)(2,1)} fusion(bf16[512,2048]{1,0:T(8,128)(2,1)} %bitcast.94, bf16[1,1024,2048]{2,1,0:T(8,128)(2,1)} %param.18), kind=kOutput, calls=%fused_computation.16 | convolution fusion | flops 2148007936 | bytes 7340032 | tf_op jit(solution)/shard_map/dot_general | solution.py:411
  79.2 43.5 %shard_map.159 = bf16[4,128,1024]{2,1,0:T(8,128)(2,1)} custom-call(bf16[4,128,1024]{2,1,0:T(8,128)(2,1)} %bitcast.105, bf16[128,1024]{1,0:T(8,128)(2,1)} %constant_dynamic-slice_fusion.2.refs_1_), custom_call_target="tpu_custom_call" | custom-call | tf_op jit(solution)/shard_map/pallas_call | solution.py:354
  122.8 1.7 constant_dynamic-slice_fusion.refs_2_
  124.4 1.6 fusion.2
  126.0 0.6 broadcast_in_dim.111.refs_1_
  126.7 5.9 %convolution_convert_fusion.2 = bf16[512,2048]{1,0:T(8,128)(2,1)} fusion(bf16[512,1024]{1,0:T(8,128)(2,1)S(1)} %bitcast.103, bf16[1,1024,2048]{2,1,0:T(8,128)(2,1)} %param.17), kind=kOutput, calls=%fused_computation.4 | convolution fusion | flops 2148532224 | bytes 7340032 | tf_op jit(solution)/shard_map/dot_general | solution.py:411
  132.5 4.4 %shard_map.160 = (bf16[2,128,2048]{2,1,0:T(8,128)(2,1)}, f32[2,8,128]{2,1,0:T(8,128)}) custom-call(bf16[2,2,128,2048]{3,2,1,0:T(8,128)(2,1)} %bitcast.96, f32[2,2,8,128]{3,2,1,0:T(8,128)} %broadcast_in_dim.111.refs_1_), custom_call_target="tpu_custom_call" | custom-call | tf_op jit(solution)/shard_map/pallas_call | solution.py:61
  137.0 0.0 copy-start.6
  137.0 0.0 copy-start.2
  137.0 0.0 copy-start.4
  137.0 3.0 fusion.3.refs_0_
  140.0 0.0 copy-done.6
  140.0 0.6 broadcast_add_fusion.refs_1_
  140.6 15.4 %shard_map.161 = (bf16[1,128,2048]{2,1,0:T(8,128)(2,1)}, f32[1,8,128]{2,1,0:T(8,128)}) custom-call(bf16[2,128,2048]{2,1,0:T(8,128)(2,1)} %fusion.3.refs_0_, f32[2,8,128]{2,1,0:T(8,128)} %broadcast_add_fusion.refs_1_), custom_call_target="tpu_custom_call" | custom-call | tf_op jit(solution)/shard_map/pallas_call | solution.py:61
  156.1 0.7 dynamic-slice_add_fusion
  156.8 0.0 copy-done.2
  156.8 0.0 copy-done.4
  156.8 3.0 fusion.5
  159.8 0.6 pad_maximum_fusion.refs_1_
  160.4 16.2 %shard_map.162 = (bf16[2,2,128,2048]{3,2,1,0:T(8,128)(2,1)}, f32[2,2,16,128]{3,2,1,0:T(8,128)}) custom-call(bf16[128,2048]{1,0:T(8,128)(2,1)} %get-tuple-element.63.refs_0_, f32[16,128]{1,0:T(8,128)} %pad_maximum_fusion.refs_1_), custom_call_target="tpu_custom_call" | custom-call | tf_op jit(solution)/shard_map/pallas_call | solution.py:229
  176.7 6.2 %convolution_convert_fusion.3 = bf16[512,1024]{1,0:T(8,128)(2,1)} fusion(bf16[512,2048]{1,0:T(8,128)(2,1)} %bitcast.126, bf16[1,1024,2048]{2,1,0:T(8,128)(2,1)} %param.17), kind=kOutput, calls=%fused_computation.15 | convolution fusion | flops 2148007936 | bytes 7340032 | tf_op jit(solution)/shard_map/dot_general | solution.py:411
  182.8 0.9 slice.21
  183.7 0.7 fusion.13
  184.4 0.1 fusion.8
  184.5 0.7 broadcast_in_dim.115.refs_4_
  185.2 0.7 broadcast_in_dim.114.refs_3_
  185.9 0.9 broadcast_select_fusion.1.refs_6_
  186.8 63.7 %shard_map.163 = (bf16[4,128,1024]{2,1,0:T(8,128)(2,1)}, bf16[2,2,128,2048]{3,2,1,0:T(8,128)(2,1)}) custom-call(bf16[4,128,1024]{2,1,0:T(8,128)(2,1)} %bitcast.104, bf16[128,1024]{1,0:T(8,128)(2,1)} %constant_dynamic-slice_fusion.2.refs_1_, bf16[128,1024]{1,0:T(8,128)(2,1)} %constant_dynamic-slice_fusion.refs_2_, f32[128,128]{1,0:T(8,128)} %broadcast_in_dim.114.refs_3_, ...), custom_call_target="tpu_custom_call" | custom-call | tf_op jit(solution)/shard_map/pallas_call | solution.py:354
  250.5 0.0 copy-done.3
  250.5 0.0 copy-start.5
  250.5 3.2 %bitcast_select_fusion.hid_ref = bf16[512,2048]{1,0:T(8,128)(2,1)} fusion(bf16[2,2,128,2048]{3,2,1,0:T(8,128)(2,1)} %get-tuple-element.51, pred[]{:T(512)S(6)} %eq.44, bf16[2,2,128,2048]{3,2,1,0:T(8,128)(2,1)S(1)} %copy-done.3), kind=kLoop, calls=%fused_computation.13 | loop fusion | flops 1048576 | bytes 6291457 | tf_op jit(solution)/shard_map/jit(_where)/select_n | solution.py:628
  253.7 0.0 copy-done.5
  253.7 1.2 bitcast_select_fusion.1.refs_0_
  255.0 28.0 %shard_map.164 = bf16[2,2,512,1024]{3,2,1,0:T(8,128)(2,1)} custom-call(bf16[512,1024]{1,0:T(8,128)(2,1)} %bitcast_select_fusion.1.refs_0_), custom_call_target="tpu_custom_call" | custom-call | tf_op jit(solution)/shard_map/pallas_call | solution.py:229
  283.0 0.0 copy-start.1
  283.0 27.2 %shard_map.165 = (f32[8,512,512]{2,1,0:T(8,128)}, f32[8,512,512]{2,1,0:T(8,128)}, bf16[8,512,512]{2,1,0:T(8,128)(2,1)}, bf16[8,512,512]{2,1,0:T(8,128)(2,1)}, bf16[8,512,512]{2,1,0:T(8,128)(2,1)}) custom-call(s32[8]{0:T(128)} %get-tuple-element.70.row_ref, s32[8]{0:T(128)} %get-tuple-element.69.col_ref, s32[8]{0:T(128)} %get-tuple-element.58.due_ref, ...), custom_call_target="tpu_custom_call" | custom-call | tf_op jit(solution)/shard_map/pallas_call | solution.py:478
  (14 shorter events, 0.1 us)
Async XLA Ops:
  0.6 4.0 %copy-start = (f32[1,4096]{1,0:T(1,128)S(1)}, f32[1,4096]{1,0:T(1,128)}, u32[]{:S(2)}) copy-start(f32[1,4096]{1,0:T(1,128)} %param.16) | copy-start | bytes 49156
  34.1 2.6 copy-start.7
  137.0 3.1 copy-start.6
  137.0 19.8 %copy-start.2 = (bf16[2,128,2048]{2,1,0:T(8,128)(2,1)S(1)}, bf16[2,128,2048]{2,1,0:T(8,128)(2,1)}, u32[]{:S(2)}) copy-start(bf16[2,128,2048]{2,1,0:T(8,128)(2,1)} %fusion.4.refs_0_) | copy-start | bytes 3145732
  137.0 19.8 %copy-start.4 = (bf16[1,128,2048]{2,1,0:T(8,128)(2,1)S(1)}, bf16[1,128,2048]{2,1,0:T(8,128)(2,1)}, u32[]{:S(2)}) copy-start(bf16[1,128,2048]{2,1,0:T(8,128)(2,1)} %get-tuple-element.43) | copy-start | bytes 1572868
  182.8 67.7 %copy-start.3 = (bf16[2,2,128,2048]{3,2,1,0:T(8,128)(2,1)S(1)}, bf16[2,2,128,2048]{3,2,1,0:T(8,128)(2,1)}, u32[]{:S(2)}) copy-start(bf16[2,2,128,2048]{3,2,1,0:T(8,128)(2,1)} %shard_map.158) | copy-start | bytes 6291460
  250.5 3.2 %copy-start.5 = (bf16[4,128,1024]{2,1,0:T(8,128)(2,1)S(1)}, bf16[4,128,1024]{2,1,0:T(8,128)(2,1)}, u32[]{:S(2)}) copy-start(bf16[4,128,1024]{2,1,0:T(8,128)(2,1)} %get-tuple-element.52) | copy-start | bytes 3145732
  283.0 27.2 %copy-start.1 = (f32[1,4096]{1,0:T(1,128)S(1)}, f32[1,4096]{1,0:T(1,128)}, u32[]{:S(2)}) copy-start(f32[1,4096]{1,0:T(1,128)} %param.16) | copy-start | bytes 49156

commit v2 on v1

--- a/solution.py
+++ b/solution.py
@@ -264,7 +264,7 @@
         far = 1 - section
         ring = [lax.rem(me + step, size) for step in range(size)]
         greet = [{"mp": ring[step]} for step in range(1, size)]
-        greet += [{"section": far, "mp": other} for other in ring]
+        greet += [{"section": far}]
         if has_aside:
             aside_greet, begin, finish = gather_parts(aside_in, aside_out, refs)
             greet += aside_greet
@@ -292,15 +292,27 @@
                 device_id_type=MESH,
             )
 
-        def far_copy(piece, step):
-            at = piece * size + step
+        def far_copy(piece):
+            at = piece * size
             window = pl.ds(piece * rows, rows)
             return pltpu.make_async_remote_copy(
                 src_ref=ready.at[window],
                 dst_ref=out_ref.at[me, window],
                 send_sem=far_send.at[at],
                 recv_sem=far_recv.at[at],
-                device_id={"section": far, "mp": ring[step]},
+                device_id={"section": far},
+                device_id_type=MESH,
+            )
+
+        def onward_copy(piece, step):
+            at = piece * size + step
+            window = pl.ds(piece * rows, rows)
+            return pltpu.make_async_remote_copy(
+                src_ref=out_ref.at[me, window],
+                dst_ref=out_ref.at[me, window],
+                send_sem=far_send.at[at],
+                recv_sem=far_recv.at[at],
+                device_id={"mp": ring[step]},
                 device_id_type=MESH,
             )
 
@@ -333,21 +345,23 @@
                     ref[window, :] if ref.shape[0] == share else ref[...] for ref in operand_refs
                 ]
                 ready[window, :] = finish_rows(total, side_total, *cut).astype(ready.dtype)
-                for step in range(size):
-                    far_copy(piece, step).start()
+                far_copy(piece).start()
             if has_aside:
                 finish()
             for piece in range(pieces):
                 for step in range(1, size):
                     sum_copy(piece, step).wait_send()
-                for step in range(size):
-                    far_copy(piece, step).wait_send()
+                far_copy(piece).wait_send()
 
         @pl.when(section != sender)
         def _():
             for piece in range(pieces):
-                for step in range(size):
-                    far_copy(piece, step).wait_recv()
+                far_copy(piece).wait_recv()
+                for step in range(1, size):
+                    onward_copy(piece, step).start()
+            for piece in range(pieces):
+                for step in range(1, size):
+                    onward_copy(piece, step).wait()
 
     dma = pltpu.SemaphoreType.DMA
     inputs = [product] + list(operands) + [x for x in (side, aside) if x is not None]

time: 313 us -> 295 us (0.942)
  Pallas kernels: 251 us -> 231 us
    pallas_call x2, Pallas kernels: 107 us -> 87.7 us  [relay(): pl.pallas_call(kernel, out_shape=[jax.ShapeDtypeStruct(product.shape, jnp...]
where the time goes in v2:
time: 295 us; the launch traced here: 290 us
  Pallas kernels  231 us (78%)
  other arithmetic  25 us (8%)
  matrix products  22.7 us (8%)
  local copies, waits for them, and re-layouts  9.89 us (3%)
    pallas_call x2, Pallas kernels, relay(): pl.pallas_call(kernel, out_shape=[jax.ShapeDtypeStruct(product.shape, jnp...  87.7 us
    pallas_call x3, Pallas kernels, gather_dp(): pl.pallas_call(kernel, out_shape=shapes, in_specs=[pl.BlockSpec(memory_sp...  61.4 us
    pallas_call x5, Pallas kernels, exchange(): pl.pallas_call(kernel, out_shape=[jax.ShapeDtypeStruct(out_lead + src.sha...  55.4 us
    pallas_call x1, Pallas kernels, precondition(): pl.pallas_call(kernel, grid_spec=pltpu.PrefetchScalarGridSpec(num_scalar_...  26.6 us
    dot_general x4, matrix products, matmul(): lax.dot_general(left, right, (((left_dim,), (right_dim,)), ((), ())), pre...  22.7 us

profile of v2, /device:TPU:0, one launch (start us, length us, event | category | flops | bytes accessed | tf_op | source)
XLA Modules:
  0.0 290.4 jit_solution(15107113746232260877)
XLA Ops:
  0.6 0.0 copy-start
  1.4 0.8 dynamic-slice_compare_fusion
  2.1 0.1 copy.27
  2.2 0.1 eq.43
  2.3 0.8 constant_dynamic-slice_fusion.5
  3.1 0.1 copy.26
  3.2 0.1 eq.37
  3.3 0.8 select_reduce_fusion
  4.0 0.6 and_select_fusion
  4.6 0.0 copy-done
  4.6 1.3 broadcast_select_fusion
  6.0 0.8 reshape.179
  6.8 1.3 copy.35
  8.1 16.0 %shard_map.155 = bf16[4,128,1024]{2,1,0:T(8,128)(2,1)S(1)} custom-call(bf16[4,128,1024]{2,1,0:T(8,128)(2,1)} %bitcast.102), custom_call_target="tpu_custom_call" | custom-call | tf_op jit(solution)/shard_map/pallas_call | solution.py:61
  24.1 0.3 multiply_reduce_fusion
  24.4 0.6 broadcast_in_dim.109.refs_1_
  25.0 0.7 constant_dynamic-slice_fusion.2.refs_1_
  25.7 4.5 %conditional.1 = (bf16[2,2,128,2048]{3,2,1,0:T(8,128)(2,1)S(1)}) conditional(s32[]{:T(128)} %convert_element_type.113, (bf16[512,1024]{1,0:T(8,128)(2,1)S(1)}, bf16[1024,2048]{1,0:T(8,128)(2,1)}) %tuple.31, (bf16[512,1024]{1,0:T(8,128)(2,1)S(1)}, f32[1024]{0:T(1024)S(1)}, bf16[1024,2048]{1,0:T(8,128)(2,1)}) %tuple.32), branch_computations={%region_2.3_spmd, %region_3.4_spmd} | conditional | flops 2150105088 | bytes 7344136 | solution.py:569
  25.7 4.5 %convolution_convert_fusion.1 = bf16[512,2048]{1,0:T(8,128)(2,1)S(1)} fusion(bf16[1024,2048]{1,0:T(8,128)(2,1)} %get-tuple-element.18, bf16[512,1024]{1,0:T(8,128)(2,1)S(1)} %get-tuple-element.16, f32[1024]{0:T(1024)S(1)} %get-tuple-element.17), kind=kOutput, calls=%fused_computation.1 | convolution fusion | flops 2150105088 | bytes 7344128 | tf_op jit(solution)/shard_map/cond/branch_1_fun/dot_general | solution.py:425
  30.2 3.9 %shard_map.156 = (bf16[2,128,2048]{2,1,0:T(8,128)(2,1)}, f32[2,8,128]{2,1,0:T(8,128)}) custom-call(bf16[2,2,128,2048]{3,2,1,0:T(8,128)(2,1)S(1)} %get-tuple-element.71.refs_0_, f32[2,2,8,128]{3,2,1,0:T(8,128)} %broadcast_in_dim.109.refs_1_), custom_call_target="tpu_custom_call" | custom-call | tf_op jit(solution)/shard_map/pallas_call | solution.py:61
  34.1 0.0 copy-start.7
  34.1 2.6 fusion.4.refs_0_
  36.7 0.0 copy-done.7
  36.7 0.6 broadcast_add_fusion.1.refs_1_
  37.3 15.7 %shard_map.157 = (bf16[1,128,2048]{2,1,0:T(8,128)(2,1)}, f32[1,8,128]{2,1,0:T(8,128)}) custom-call(bf16[2,128,2048]{2,1,0:T(8,128)(2,1)} %fusion.4.refs_0_, f32[2,8,128]{2,1,0:T(8,128)} %broadcast_add_fusion.1.refs_1_), custom_call_target="tpu_custom_call" | custom-call | tf_op jit(solution)/shard_map/pallas_call | solution.py:61
  53.0 0.7 dynamic-slice_add_fusion.1
  53.7 2.4 multiply_convert_fusion.3.refs_0_
  56.1 17.0 %shard_map.158 = bf16[2,2,128,2048]{3,2,1,0:T(8,128)(2,1)} custom-call(bf16[128,2048]{1,0:T(8,128)(2,1)} %multiply_convert_fusion.3.refs_0_), custom_call_target="tpu_custom_call" | custom-call | tf_op jit(solution)/shard_map/pallas_call | solution.py:229
  73.1 6.2 %convolution_convert_fusion.4 = bf16[512,1024]{1,0:T(8,128)(2,1)} fusion(bf16[512,2048]{1,0:T(8,128)(2,1)} %bitcast.94, bf16[1,1024,2048]{2,1,0:T(8,128)(2,1)} %param.18), kind=kOutput, calls=%fused_computation.16 | convolution fusion | flops 2148007936 | bytes 7340032 | tf_op jit(solution)/shard_map/dot_general | solution.py:425
  79.2 30.5 %shard_map.159 = bf16[4,128,1024]{2,1,0:T(8,128)(2,1)} custom-call(bf16[4,128,1024]{2,1,0:T(8,128)(2,1)} %bitcast.105, bf16[128,1024]{1,0:T(8,128)(2,1)} %constant_dynamic-slice_fusion.2.refs_1_), custom_call_target="tpu_custom_call" | custom-call | tf_op jit(solution)/shard_map/pallas_call | solution.py:368
  109.8 1.7 constant_dynamic-slice_fusion.refs_2_
  111.5 1.6 fusion.2
  113.1 0.6 broadcast_in_dim.111.refs_1_
  113.7 5.9 %convolution_convert_fusion.2 = bf16[512,2048]{1,0:T(8,128)(2,1)} fusion(bf16[512,1024]{1,0:T(8,128)(2,1)S(1)} %bitcast.103, bf16[1,1024,2048]{2,1,0:T(8,128)(2,1)} %param.17), kind=kOutput, calls=%fused_computation.4 | convolution fusion | flops 2148532224 | bytes 7340032 | tf_op jit(solution)/shard_map/dot_general | solution.py:425
  119.6 4.4 %shard_map.160 = (bf16[2,128,2048]{2,1,0:T(8,128)(2,1)}, f32[2,8,128]{2,1,0:T(8,128)}) custom-call(bf16[2,2,128,2048]{3,2,1,0:T(8,128)(2,1)} %bitcast.96, f32[2,2,8,128]{3,2,1,0:T(8,128)} %broadcast_in_dim.111.refs_1_), custom_call_target="tpu_custom_call" | custom-call | tf_op jit(solution)/shard_map/pallas_call | solution.py:61
  124.0 0.0 copy-start.6
  124.0 0.0 copy-start.2
  124.0 0.0 copy-start.4
  124.1 3.0 %fusion.3.refs_0_ = bf16[2,128,2048]{2,1,0:T(8,128)(2,1)} fusion(bf16[2,128,2048]{2,1,0:T(8,128)(2,1)} %get-tuple-element.45, bf16[2,2,128,2048]{3,2,1,0:T(8,128)(2,1)} %bitcast.97, s32[]{:T(128)S(6)} %select_n.117), kind=kLoop, calls=%fused_computation.10 | loop fusion | flops 2097152 | bytes 3145732 | tf_op jit(solution)/shard_map/convert_element_type | solution.py:407
  127.1 0.0 copy-done.6
  127.1 0.6 broadcast_add_fusion.refs_1_
  127.7 15.4 %shard_map.161 = (bf16[1,128,2048]{2,1,0:T(8,128)(2,1)}, f32[1,8,128]{2,1,0:T(8,128)}) custom-call(bf16[2,128,2048]{2,1,0:T(8,128)(2,1)} %fusion.3.refs_0_, f32[2,8,128]{2,1,0:T(8,128)} %broadcast_add_fusion.refs_1_), custom_call_target="tpu_custom_call" | custom-call | tf_op jit(solution)/shard_map/pallas_call | solution.py:61
  143.1 0.7 dynamic-slice_add_fusion
  143.8 0.0 copy-done.2
  143.8 0.0 copy-done.4
  143.9 3.0 %fusion.5 = (f32[128]{0:T(128)S(1)}, bf16[128,2048]{1,0:T(8,128)(2,1)}, bf16[128,2048]{1,0:T(8,128)(2,1)}) fusion(bf16[1,128,2048]{2,1,0:T(8,128)(2,1)} %get-tuple-element.47, bf16[2,128,2048]{2,1,0:T(8,128)(2,1)} %fusion.3.refs_0_, s32[]{:T(128)S(6)} %select_n.119, f32[128]{0:T(128)S(1)} %rsqrt_bitcast_fusion, bf16[1,128,2048]{2,1,0:T(8,128)(2,1)S(1)} %copy-done.4, ...), kind=kLoop, calls=%fused_computation.20 | loop fusion | flops 5504896 | bytes 3146756 | tf_op jit(solution)/shard_map/reduce_sum | solution.py:602
  146.9 0.6 pad_maximum_fusion.refs_1_
  147.5 16.2 %shard_map.162 = (bf16[2,2,128,2048]{3,2,1,0:T(8,128)(2,1)}, f32[2,2,16,128]{3,2,1,0:T(8,128)}) custom-call(bf16[128,2048]{1,0:T(8,128)(2,1)} %get-tuple-element.63.refs_0_, f32[16,128]{1,0:T(8,128)} %pad_maximum_fusion.refs_1_), custom_call_target="tpu_custom_call" | custom-call | tf_op jit(solution)/shard_map/pallas_call | solution.py:229
  163.7 6.2 %convolution_convert_fusion.3 = bf16[512,1024]{1,0:T(8,128)(2,1)} fusion(bf16[512,2048]{1,0:T(8,128)(2,1)} %bitcast.126, bf16[1,1024,2048]{2,1,0:T(8,128)(2,1)} %param.17), kind=kOutput, calls=%fused_computation.15 | convolution fusion | flops 2148007936 | bytes 7340032 | tf_op jit(solution)/shard_map/dot_general | solution.py:425
  169.9 0.9 slice.21
  170.7 0.7 fusion.13
  171.5 0.1 fusion.8
  171.6 0.7 broadcast_in_dim.115.refs_4_
  172.3 0.7 broadcast_in_dim.114.refs_3_
  173.0 0.9 broadcast_select_fusion.1.refs_6_
  173.8 57.1 %shard_map.163 = (bf16[4,128,1024]{2,1,0:T(8,128)(2,1)}, bf16[2,2,128,2048]{3,2,1,0:T(8,128)(2,1)}) custom-call(bf16[4,128,1024]{2,1,0:T(8,128)(2,1)} %bitcast.104, bf16[128,1024]{1,0:T(8,128)(2,1)} %constant_dynamic-slice_fusion.2.refs_1_, bf16[128,1024]{1,0:T(8,128)(2,1)} %constant_dynamic-slice_fusion.refs_2_, f32[128,128]{1,0:T(8,128)} %broadcast_in_dim.114.refs_3_, ...), custom_call_target="tpu_custom_call" | custom-call | tf_op jit(solution)/shard_map/pallas_call | solution.py:368
  231.0 0.0 copy-done.3
  231.0 0.0 copy-start.5
  231.0 3.2 %bitcast_select_fusion.hid_ref = bf16[512,2048]{1,0:T(8,128)(2,1)} fusion(bf16[2,2,128,2048]{3,2,1,0:T(8,128)(2,1)} %get-tuple-element.51, pred[]{:T(512)S(6)} %eq.44, bf16[2,2,128,2048]{3,2,1,0:T(8,128)(2,1)S(1)} %copy-done.3), kind=kLoop, calls=%fused_computation.13 | loop fusion | flops 1048576 | bytes 6291457 | tf_op jit(solution)/shard_map/jit(_where)/select_n | solution.py:642
  234.2 0.0 copy-done.5
  234.2 1.2 bitcast_select_fusion.1.refs_0_
  235.5 28.2 %shard_map.164 = bf16[2,2,512,1024]{3,2,1,0:T(8,128)(2,1)} custom-call(bf16[512,1024]{1,0:T(8,128)(2,1)} %bitcast_select_fusion.1.refs_0_), custom_call_target="tpu_custom_call" | custom-call | tf_op jit(solution)/shard_map/pallas_call | solution.py:229
  263.7 0.0 copy-start.1
  263.7 26.6 %shard_map.165 = (f32[8,512,512]{2,1,0:T(8,128)}, f32[8,512,512]{2,1,0:T(8,128)}, bf16[8,512,512]{2,1,0:T(8,128)(2,1)}, bf16[8,512,512]{2,1,0:T(8,128)(2,1)}, bf16[8,512,512]{2,1,0:T(8,128)(2,1)}) custom-call(s32[8]{0:T(128)} %get-tuple-element.70.row_ref, s32[8]{0:T(128)} %get-tuple-element.69.col_ref, s32[8]{0:T(128)} %get-tuple-element.58.due_ref, ...), custom_call_target="tpu_custom_call" | custom-call | tf_op jit(solution)/shard_map/pallas_call | solution.py:492
  (14 shorter events, 0.1 us)
Async XLA Ops:
  0.6 4.0 %copy-start = (f32[1,4096]{1,0:T(1,128)S(1)}, f32[1,4096]{1,0:T(1,128)}, u32[]{:S(2)}) copy-start(f32[1,4096]{1,0:T(1,128)} %param.16) | copy-start | bytes 49156
  34.1 2.6 copy-start.7
  124.0 3.1 %copy-start.6 = (f32[2,8,128]{2,1,0:T(8,128)S(1)}, f32[2,8,128]{2,1,0:T(8,128)}, u32[]{:S(2)}) copy-start(f32[2,8,128]{2,1,0:T(8,128)} %get-tuple-element.46) | copy-start | bytes 24580
  124.0 19.8 %copy-start.2 = (bf16[2,128,2048]{2,1,0:T(8,128)(2,1)S(1)}, bf16[2,128,2048]{2,1,0:T(8,128)(2,1)}, u32[]{:S(2)}) copy-start(bf16[2,128,2048]{2,1,0:T(8,128)(2,1)} %fusion.4.refs_0_) | copy-start | bytes 3145732
  124.0 19.8 %copy-start.4 = (bf16[1,128,2048]{2,1,0:T(8,128)(2,1)S(1)}, bf16[1,128,2048]{2,1,0:T(8,128)(2,1)}, u32[]{:S(2)}) copy-start(bf16[1,128,2048]{2,1,0:T(8,128)(2,1)} %get-tuple-element.43) | copy-start | bytes 1572868
  169.9 61.1 %copy-start.3 = (bf16[2,2,128,2048]{3,2,1,0:T(8,128)(2,1)S(1)}, bf16[2,2,128,2048]{3,2,1,0:T(8,128)(2,1)}, u32[]{:S(2)}) copy-start(bf16[2,2,128,2048]{3,2,1,0:T(8,128)(2,1)} %shard_map.158) | copy-start | bytes 6291460
  231.0 3.2 %copy-start.5 = (bf16[4,128,1024]{2,1,0:T(8,128)(2,1)S(1)}, bf16[4,128,1024]{2,1,0:T(8,128)(2,1)}, u32[]{:S(2)}) copy-start(bf16[4,128,1024]{2,1,0:T(8,128)(2,1)} %get-tuple-element.52) | copy-start | bytes 3145732
  263.7 26.6 %copy-start.1 = (f32[1,4096]{1,0:T(1,128)S(1)}, f32[1,4096]{1,0:T(1,128)}, u32[]{:S(2)}) copy-start(f32[1,4096]{1,0:T(1,128)} %param.16) | copy-start | bytes 49156
